TPU v7x, 32 devices: a whole 2x2x4 slice. The times are simulated.
32 devices in a mesh: expert: 16 (over z, y, x), replica: 2 (over core).
Axes of the slice: x: 2, y: 2, z: 4, core: 2. Of those that a mesh axis runs over, the one named last changes fastest.
Arguments:
- tokens: bfloat16 [1024, 7168], P('expert', 'replica'), may hold values from -6 to 6
- routes: int32 [1024, 8], P('expert'), may hold values from 0 to 15, all different within a row; in each aligned block of 64 rows (0 to 63, 64 to 127, ...) at most 64 rows name the same one
- route_scores: float32 [1024, 8], P('expert'), may hold values from 0.05 to 1
- placement: int32 [16], replicated, may hold values from 0 to 15, each once
- w_in: bfloat16 [16, 7168, 2, 1024], P('expert', 'replica'), may hold values from -0.0625 to 0.0625
- w_out: bfloat16 [16, 1024, 7168], P('expert', None, 'replica'), may hold values from -0.1875 to 0.1875
Outputs:
- mixed: bfloat16 [1024, 7168], P('expert', 'replica')
Inputs may be any that keep to these rules, and one draw needn't show every extreme that they name: `routes`: each row names 8 different logical experts. Among the 64 rows of each aligned block (the tokens of one index of the expert axis) no expert is named by more than 64 rows, a bound that some block reaches. `placement`: A permutation of the physical slots.
All inputs are finite; a program needn't handle non-finite values.
Results may differ from a plain program's by a relative error of at most 0.0057.
Values may be sent and summed in bfloat16 or wider, within the bound.
A program may use at most 128 MiB of HBM per device.

v0:
```python
import jax
import jax.numpy as jnp
from jax import lax
from jax.sharding import PartitionSpec as P


def packed(tokens, routes, route_scores, placement, w_in, w_out):
    tok_rows, feature_cols = tokens.shape
    route_count = routes.shape[1]
    experts = placement.shape[0]
    hidden_units = w_in.shape[3]
    capacity = min(tok_rows, max(2, 2 * tok_rows * route_count // experts))
    slot_total = experts * capacity
    expert_ids = jnp.arange(experts, dtype=jnp.int32)
    route_table = routes[:, :, None] == expert_ids
    physical = jnp.sum(jnp.where(route_table, placement, 0), axis=-1)
    flat_slots = physical.reshape(-1)
    onehot = (flat_slots[:, None] == expert_ids).astype(jnp.int32)
    earlier = jnp.sum((jnp.cumsum(onehot, axis=0) - onehot) * onehot, axis=1)
    position = (flat_slots * capacity + earlier).reshape(tok_rows, route_count)
    slot_index = jnp.arange(slot_total, dtype=jnp.int32)
    placing = jnp.any(position[None, :, :] == slot_index[:, None, None], axis=-1).astype(
        jnp.bfloat16
    )
    outgoing = jnp.dot(placing, tokens, preferred_element_type=jnp.float32).astype(jnp.bfloat16)
    incoming = lax.all_to_all(outgoing, "expert", split_axis=0, concat_axis=0, tiled=True)
    weights_in = w_in[0].reshape(feature_cols, 2 * hidden_units)
    weights_out = w_out[0]
    partial_value = jnp.dot(incoming, weights_in, preferred_element_type=jnp.float32)
    partial_value = partial_value.reshape(slot_total, 2, hidden_units)
    shares = lax.psum_scatter(partial_value, "replica", scatter_dimension=2, tiled=True)
    active = (jax.nn.silu(shares[:, 0]) * shares[:, 1]).astype(jnp.bfloat16)
    result = jnp.dot(
        lax.all_gather(active, "replica", axis=1, tiled=True),
        weights_out,
        preferred_element_type=jnp.float32,
    )
    expert_out = result.astype(jnp.bfloat16)
    returned = lax.all_to_all(expert_out, "expert", split_axis=0, concat_axis=0, tiled=True)
    route_weight = 2.5 * route_scores / jnp.sum(route_scores, axis=1, keepdims=True)
    picked = returned[position.reshape(-1)].reshape(tok_rows, route_count, feature_cols)
    mixed = jnp.sum(picked.astype(jnp.float32) * route_weight[:, :, None], axis=1)
    return mixed.astype(jnp.bfloat16)


def expert_weights(routes, route_scores, placement):
    experts = placement.shape[0]
    expert_ids = jnp.arange(experts, dtype=jnp.int32)
    physical = jnp.sum(jnp.where(routes[:, :, None] == expert_ids, placement, 0), axis=-1)
    route_weight = 2.5 * route_scores / jnp.sum(route_scores, axis=1, keepdims=True)
    return jnp.sum(
        jnp.where(physical[:, :, None] == expert_ids, route_weight[:, :, None], 0.0), axis=1
    )


def dense(tokens, routes, route_scores, placement, w_in, w_out):
    feature_cols = tokens.shape[1]
    hidden_units = w_in.shape[3]
    table = expert_weights(routes, route_scores, placement)
    mine = lax.all_to_all(table, "expert", split_axis=1, concat_axis=0, tiled=True)
    incoming = lax.all_gather(tokens, "expert", axis=0, tiled=True)
    rows = incoming.shape[0]
    weights_in = w_in[0].reshape(feature_cols, 2 * hidden_units)
    partial_value = jnp.dot(incoming, weights_in, preferred_element_type=jnp.float32)
    partial_value = partial_value.reshape(rows, 2, hidden_units)
    shares = lax.psum_scatter(partial_value, "replica", scatter_dimension=2, tiled=True)
    active = (jax.nn.silu(shares[:, 0]) * shares[:, 1]).astype(jnp.bfloat16)
    result = jnp.dot(
        lax.all_gather(active, "replica", axis=1, tiled=True),
        w_out[0],
        preferred_element_type=jnp.float32,
    )
    weighted = (result.astype(jnp.bfloat16).astype(jnp.float32) * mine).astype(jnp.bfloat16)
    return lax.psum_scatter(weighted, "expert", scatter_dimension=0, tiled=True)


def on_device(tokens, routes, route_scores, placement, w_in, w_out):
    tok_rows = tokens.shape[0]
    if 2 * tok_rows * routes.shape[1] // placement.shape[0] >= tok_rows:
        return dense(tokens, routes, route_scores, placement, w_in, w_out)
    return packed(tokens, routes, route_scores, placement, w_in, w_out)


def solution(mesh):
    in_specs = (
        P("expert", "replica"),
        P("expert", None),
        P("expert", None),
        P(),
        P("expert", "replica", None, None),
        P("expert", None, "replica"),
    )
    out_specs = P("expert", "replica")
    return jax.shard_map(
        on_device, mesh=mesh, in_specs=in_specs, out_specs=out_specs, check_vma=False
    )
```

profile of v0, /device:TPU:10, one launch (start us, length us, event | category | flops | bytes accessed | tf_op | source)
XLA Modules:
  0.0 345.8 jit_solution(17655661760736529164)
XLA Ops:
  6.5 0.0 all-gather.3.cloned.1.call-start
  6.5 0.7 all-gather.3.cloned.1.call-update
  7.3 0.0 reduce-scatter.3.cloned.1.call-start
  7.3 16.1 %copy.18 = bf16[448,8,2,1024]{3,1,2,0:T(8,128)(2,1)} copy(bf16[448,8,2,1024]{3,2,1,0:T(2,128)(2,1)} %bitcast.32) | data formatting | bytes 29360128
  23.4 18.9 %copy.16 = bf16[2048,3584]{1,0:T(8,128)(2,1)} copy(bf16[2048,3584]{0,1:T(8,128)(2,1)} %bitcast.31) | data formatting | bytes 29360128 | tf_op jit(solution)/shard_map/dot_general | solution.py:64
  42.3 71.1 %all-gather.3.cloned.1.call-done = bf16[1024,3584]{1,0:T(8,128)(2,1)} async-done(((bf16[64,3584]{1,0:T(8,128)(2,1)}), bf16[1024,3584]{1,0:T(8,128)(2,1)}) %all-gather.3.cloned.1.call-update) | async-done | bytes 7340048 | tf_op jit(solution)/shard_map/all_gather | solution.py:61
  113.4 21.6 %fusion.3 = f32[1024,2,1024]{2,0,1:T(8,128)} fusion(bf16[2,1024,3584]{2,1,0:T(8,128)(2,1)} %bitcast.33, bf16[1024,3584]{1,0:T(8,128)(2,1)} %all-gather.3.cloned.1.call-done), kind=kOutput, calls=%fused_computation.3 | convolution fusion | flops 15032385536 | bytes 30408704 | tf_op jit(solution)/shard_map/dot_general | solution.py:64
  135.0 0.0 copy-start
  135.0 0.0 copy-start.1
  135.0 0.0 reduce-scatter.3.cloned.1.call-update
  135.0 0.0 all-gather.5.cloned.1.call-start
  135.0 15.7 %reduce-scatter.3.cloned.1.call-done = f32[1024,2,512]{2,0,1:T(8,128)} async-done(((f32[1024,2,1024]{2,0,1:T(8,128)}), f32[1024,2,512]{2,0,1:T(8,128)}) %reduce-scatter.3.cloned.1.call-update) | async-done | bytes 4194320 | tf_op jit(solution)/shard_map/reduce_scatter | solution.py:66
  150.7 3.8 %fusion.6 = bf16[1024,512]{1,0:T(8,128)(2,1)} fusion(f32[1024,2,512]{2,0,1:T(8,128)} %reduce-scatter.3.cloned.1.call-done), kind=kLoop, calls=%fused_computation.7 | loop fusion | flops 3145728 | bytes 5242880 | tf_op jit(solution)/shard_map/convert_element_type | solution.py:67
  154.5 0.0 all-gather.5.cloned.1.call-update
  154.6 0.0 reduce-scatter.5.cloned.1.call-start
  154.6 0.0 copy-done
  154.7 0.0 copy-done.1
  154.7 0.0 copy-done.2
  154.7 0.1 select_reduce_fusion.1
  154.8 11.8 %all_to_all.16 = f32[64,16,1]{0,2,1:T(1,128)S(1)} all-to-all(f32[64,16,1]{0,2,1:T(1,128)S(1)} %bitcast.34), channel_id=1, replica_groups=mesh['expert'=16,'replica'=2] {'expert'}, dimensions={1} | all-to-all | bytes 8192 | tf_op jit(solution)/shard_map/all_to_all | solution.py:60
  166.7 0.1 mul.27
  166.7 12.5 %multiply_convert_fusion = bf16[1024,3584]{1,0:T(8,128)(2,1)} fusion(bf16[1024,1024]{1,0:T(8,128)(2,1)} %all-gather.5.cloned.1.call-done, bf16[1,1024,3584]{2,1,0:T(8,128)(2,1)} %param.11, f32[1024]{0:T(1024)S(1)} %mul.27), kind=kOutput, calls=%fused_computation | convolution fusion | flops 7530872832 | bytes 16781312 | tf_op jit(solution)/shard_map/dot_general | solution.py:68
  179.2 0.0 reduce-scatter.5.cloned.1.call-update
  179.3 160.0 %reduce-scatter.5.cloned.1.call-done = bf16[64,3584]{1,0:T(8,128)(2,1)} async-done(((bf16[1024,3584]{1,0:T(8,128)(2,1)}), bf16[64,3584]{1,0:T(8,128)(2,1)}) %reduce-scatter.5.cloned.1.call-update) | async-done | bytes 458768 | tf_op jit(solution)/shard_map/reduce_scatter | solution.py:74
  (6 shorter events, 0.1 us)
Async XLA Ops:
  6.5 106.8 %all-gather.3.cloned.1.call-start = ((), (), s32[]{:S(2)}) async-start(), calls=%async_computation.3 | async-start | bytes 7798784 | tf_op jit(solution)/shard_map/all_gather | solution.py:61
  7.3 143.4 %reduce-scatter.3.cloned.1.call-start = ((), (), s32[]{:S(2)}) async-start(), calls=%async_computation.4 | async-start | bytes 12582912 | tf_op jit(solution)/shard_map/reduce_scatter | solution.py:66
  135.0 19.7 %copy-start = (f32[64,8]{0,1:T(8,128)S(1)}, f32[64,8]{0,1:T(8,128)}, u32[]{:S(2)}) copy-start(f32[64,8]{0,1:T(8,128)} %param.8) | copy-start | bytes 6148
  135.0 19.7 %copy-start.1 = (s32[64,8]{0,1:T(8,128)S(1)}, s32[64,8]{0,1:T(8,128)}, u32[]{:S(2)}) copy-start(s32[64,8]{0,1:T(8,128)} %param.7) | copy-start | bytes 6148
  135.0 19.7 %copy-start.2 = (s32[16]{0:T(128)S(1)}, s32[16]{0:T(128)}, u32[]{:S(2)}) copy-start(s32[16]{0:T(128)} %param.9) | copy-start | bytes 196
  135.0 31.7 %all-gather.5.cloned.1.call-start = ((), (), s32[]{:S(2)}) async-start(), calls=%async_computation.5 | async-start | bytes 3145728 | tf_op jit(solution)/shard_map/all_gather | solution.py:69
  154.6 184.7 %reduce-scatter.5.cloned.1.call-start = ((), (), s32[]{:S(2)}) async-start(), calls=%async_computation.6 | async-start | bytes 7798784 | tf_op jit(solution)/shard_map/reduce_scatter | solution.py:74
Sparse Core Ops, SparseCore 0:
  10.0 103.2 all-gather.2
  135.1 15.5 reduce-scatter.2
  154.7 11.7 all-gather.4
  179.4 159.8 reduce-scatter.4
where the time goes:
time: 347 us; the launch traced here: 346 us
  waiting for transfers between devices  248 us (71%)
  local copies, waits for them, and re-layouts  35.1 us (10%)
  matrix products  34.1 us (10%)
  between operations  13.2 us (4%)
  blocking collectives  11.8 us (3%)
  other arithmetic  3.98 us (1%)
    reduce_scatter x1, waiting for transfers between devices, dense(): return lax.psum_scatter(weighted, 'expert', scatter_dimension=0, tiled=True)  160 us
    all_gather x1, waiting for transfers between devices, dense(): incoming = lax.all_gather(tokens, 'expert', axis=0, tiled=True)  71.1 us
    dot_general x1, matrix products, dense(): jnp.dot(incoming, weights_in, preferred_element_type=jnp.float32)  21.6 us
    dot_general x1, local copies, waits for them, and re-layouts, dense(): jnp.dot(incoming, weights_in, preferred_element_type=jnp.float32)  18.9 us
    unnamed x7, local copies, waits for them, and re-layouts  16.1 us
    reduce_scatter x1, waiting for transfers between devices, dense(): lax.psum_scatter(partial_value, 'replica', scatter_dimension=2, tiled=True)  15.7 us
    dot_general x1, matrix products, dense(): jnp.dot(lax.all_gather(active, 'replica', axis=1, tiled=True), w_out[0],...  12.5 us
    all_to_all x1, blocking collectives, dense(): lax.all_to_all(table, 'expert', split_axis=1, concat_axis=0, tiled=True)  11.8 us
  transfers between devices with their start and end apart: 4, of which 3 were waited for; matrix products, arithmetic and copies ran while one was open for 10% of the time, Pallas kernels for 0%

commit v1 on v0

--- a/solution.py
+++ b/solution.py
@@ -2,6 +2,18 @@
 import jax.numpy as jnp
 from jax import lax
 from jax.sharding import PartitionSpec as P
+
+
+def gather_by_bits(value, axis, dim):
+    ways, here = (lax.axis_size(axis), lax.axis_index(axis))
+    grown, reach = (value, 1)
+    while reach < ways:
+        theirs = lax.ppermute(grown, axis, [(d, d ^ reach) for d in range(ways)])
+        mine_first = jnp.concatenate([grown, theirs], axis=dim)
+        theirs_first = jnp.concatenate([theirs, grown], axis=dim)
+        grown = jnp.where(here & reach == 0, mine_first, theirs_first)
+        reach = 2 * reach
+    return grown
 
 
 def packed(tokens, routes, route_scores, placement, w_in, w_out):
@@ -58,7 +70,7 @@
     hidden_units = w_in.shape[3]
     table = expert_weights(routes, route_scores, placement)
     mine = lax.all_to_all(table, "expert", split_axis=1, concat_axis=0, tiled=True)
-    incoming = lax.all_gather(tokens, "expert", axis=0, tiled=True)
+    incoming = gather_by_bits(tokens, "expert", 0)
     rows = incoming.shape[0]
     weights_in = w_in[0].reshape(feature_cols, 2 * hidden_units)
     partial_value = jnp.dot(incoming, weights_in, preferred_element_type=jnp.float32)

time: 347 us -> 485 us (1.40)
  waiting for transfers between devices: 248 us -> 370 us
  other arithmetic: 3.98 us -> 11.1 us
  starting transfers between devices: 0.12 us -> 5.31 us
    ppermute x0 -> x4, waiting for transfers between devices: none -> 192 us  [gather_by_bits(): theirs = lax.ppermute(grown, axis, [(d, d ^ reach) for d in range(ways)])]
    all_gather x1 -> x0, waiting for transfers between devices: 71.1 us -> none  [dense(): incoming = lax.all_gather(tokens, 'expert', axis=0, tiled=True)]
    select_n x0 -> x3, other arithmetic: none -> 7.08 us  [gather_by_bits(): grown = jnp.where(here & reach == 0, mine_first, theirs_first)]
    ppermute x0 -> x4, starting transfers between devices: none -> 5.22 us  [gather_by_bits(): theirs = lax.ppermute(grown, axis, [(d, d ^ reach) for d in range(ways)])]
  transfers between devices with their start and end apart: 4 -> 7, of which waited for: 3 -> 6; matrix products, arithmetic and copies ran while one was open for 10% -> 7% of each run, Pallas kernels for 0% -> 0%
where the time goes in v1:
time: 485 us; the launch traced here: 484 us
  waiting for transfers between devices  370 us (76%)
  matrix products  37.3 us (8%)
  local copies, waits for them, and re-layouts  34.9 us (7%)
  between operations  13.2 us (3%)
  blocking collectives  11.8 us (2%)
  other arithmetic  11.1 us (2%)
  starting transfers between devices  5.31 us (1%)
    ppermute x4, waiting for transfers between devices, gather_by_bits(): theirs = lax.ppermute(grown, axis, [(d, d ^ reach) for d in range(ways)])  192 us
    reduce_scatter x1, waiting for transfers between devices, dense(): return lax.psum_scatter(weighted, 'expert', scatter_dimension=0, tiled=True)  160 us
    dot_general x1, matrix products, dense(): jnp.dot(incoming, weights_in, preferred_element_type=jnp.float32)  24.8 us
    dot_general x1, local copies, waits for them, and re-layouts, dense(): jnp.dot(incoming, weights_in, preferred_element_type=jnp.float32)  18.8 us
    reduce_scatter x1, waiting for transfers between devices, dense(): lax.psum_scatter(partial_value, 'replica', scatter_dimension=2, tiled=True)  18.6 us
    unnamed x7, local copies, waits for them, and re-layouts  16 us
    dot_general x1, matrix products, dense(): jnp.dot(lax.all_gather(active, 'replica', axis=1, tiled=True), w_out[0],...  12.5 us
    all_to_all x1, blocking collectives, dense(): lax.all_to_all(table, 'expert', split_axis=1, concat_axis=0, tiled=True)  11.8 us
  transfers between devices with their start and end apart: 7, of which 6 were waited for; matrix products, arithmetic and copies ran while one was open for 7% of the time, Pallas kernels for 0%

profile of v1, /device:TPU:10, one launch (start us, length us, event | category | flops | bytes accessed | tf_op | source)
XLA Modules:
  0.0 483.8 jit_solution(5600653667757588298)
XLA Ops:
  6.5 0.5 collective-permute-start
  7.1 11.9 %collective-permute-done = bf16[64,3584]{1,0:T(8,128)(2,1)S(1)} collective-permute-done((bf16[64,3584]{1,0:T(8,128)(2,1)}, bf16[64,3584]{1,0:T(8,128)(2,1)S(1)}, u32[]{:S(2)}, u32[]{:S(2)}) %collective-permute-start) | collective-permute-done | bytes 458784 | tf_op jit(solution)/shard_map/ppermute | solution.py:11
  19.0 1.3 maximum_select_fusion.3
  20.3 1.6 collective-permute-start.1
  21.9 19.8 %collective-permute-done.1 = bf16[128,3584]{1,0:T(8,128)(2,1)} collective-permute-done((bf16[128,3584]{1,0:T(8,128)(2,1)S(1)}, bf16[128,3584]{1,0:T(8,128)(2,1)}, u32[]{:S(2)}, u32[]{:S(2)}) %collective-permute-start.1) | collective-permute-done | bytes 917536 | tf_op jit(solution)/shard_map/ppermute | solution.py:11
  41.8 1.9 maximum_select_fusion.2
  43.7 0.5 collective-permute-start.2
  44.2 39.7 %collective-permute-done.2 = bf16[256,3584]{1,0:T(8,128)(2,1)} collective-permute-done((bf16[256,3584]{1,0:T(8,128)(2,1)S(1)}, bf16[256,3584]{1,0:T(8,128)(2,1)}, u32[]{:S(2)}, u32[]{:S(2)}) %collective-permute-start.2) | collective-permute-done | bytes 1835040 | tf_op jit(solution)/shard_map/ppermute | solution.py:11
  83.9 3.9 maximum_select_fusion.1
  87.7 2.6 collective-permute-start.3
  90.3 16.0 %copy.18 = bf16[448,8,2,1024]{3,1,2,0:T(8,128)(2,1)} copy(bf16[448,8,2,1024]{3,2,1,0:T(2,128)(2,1)} %bitcast.32) | data formatting | bytes 29360128
  106.3 18.8 %copy.16 = bf16[2048,3584]{1,0:T(8,128)(2,1)} copy(bf16[2048,3584]{0,1:T(8,128)(2,1)} %bitcast.31) | data formatting | bytes 29360128 | tf_op jit(solution)/shard_map/dot_general | solution.py:76
  125.1 120.1 %collective-permute-done.3 = bf16[512,3584]{1,0:T(8,128)(2,1)} collective-permute-done((bf16[512,3584]{1,0:T(8,128)(2,1)}, bf16[512,3584]{1,0:T(8,128)(2,1)}, u32[]{:S(2)}, u32[]{:S(2)}) %collective-permute-start.3) | collective-permute-done | bytes 3670048 | tf_op jit(solution)/shard_map/ppermute | solution.py:11
  245.2 24.8 %fusion.1 = f32[1024,2,1024]{2,0,1:T(8,128)} fusion(bf16[2,1024,3584]{2,1,0:T(8,128)(2,1)} %bitcast.33, bf16[512,3584]{1,0:T(8,128)(2,1)} %collective-permute-done.3, bf16[512,3584]{1,0:T(8,128)(2,1)} %maximum_select_fusion.1, pred[]{:T(512)S(6)} %eq.38), kind=kOutput, calls=%fused_computation.4 | convolution fusion | flops 15065415680 | bytes 30408704 | tf_op jit(solution)/shard_map/dot_general | solution.py:76
  270.0 0.0 reduce-scatter.3.cloned.1.call-update
  270.0 0.0 all-gather.2.cloned.1.call-start
  270.1 18.6 %reduce-scatter.3.cloned.1.call-done = f32[1024,2,512]{2,0,1:T(8,128)} async-done(((f32[1024,2,1024]{2,0,1:T(8,128)}), f32[1024,2,512]{2,0,1:T(8,128)}) %reduce-scatter.3.cloned.1.call-update) | async-done | bytes 4194320 | tf_op jit(solution)/shard_map/reduce_scatter | solution.py:78
  288.7 3.8 fusion.13
  292.6 0.0 reduce-scatter.5.cloned.1.call-start
  292.6 0.1 select_reduce_fusion.1
  292.8 11.8 %all_to_all.16 = f32[64,16,1]{0,2,1:T(1,128)S(1)} all-to-all(f32[64,16,1]{0,2,1:T(1,128)S(1)} %bitcast.34), channel_id=1, replica_groups=mesh['expert'=16,'replica'=2] {'expert'}, dimensions={1} | all-to-all | bytes 8192 | tf_op jit(solution)/shard_map/all_to_all | solution.py:72
  304.6 0.1 mul.27
  304.7 12.5 %multiply_convert_fusion = bf16[1024,3584]{1,0:T(8,128)(2,1)} fusion(bf16[1024,1024]{1,0:T(8,128)(2,1)} %all-gather.2.cloned.1.call-done, bf16[1,1024,3584]{2,1,0:T(8,128)(2,1)} %param.11, f32[1024]{0:T(1024)S(1)} %mul.27), kind=kOutput, calls=%fused_computation | convolution fusion | flops 7530872832 | bytes 16781312 | tf_op jit(solution)/shard_map/dot_general | solution.py:80
  317.2 160.0 %reduce-scatter.5.cloned.1.call-done = bf16[64,3584]{1,0:T(8,128)(2,1)} async-done(((bf16[1024,3584]{1,0:T(8,128)(2,1)}), bf16[64,3584]{1,0:T(8,128)(2,1)}) %reduce-scatter.5.cloned.1.call-update) | async-done | bytes 458768 | tf_op jit(solution)/shard_map/reduce_scatter | solution.py:86
  (14 shorter events, 0.1 us)
Async XLA Ops:
  6.5 282.1 %reduce-scatter.3.cloned.1.call-start = ((), (), s32[]{:S(2)}) async-start(), calls=%async_computation.3 | async-start | bytes 12582912 | tf_op jit(solution)/shard_map/reduce_scatter | solution.py:78
  6.5 12.5 %collective-permute-start = (bf16[64,3584]{1,0:T(8,128)(2,1)}, bf16[64,3584]{1,0:T(8,128)(2,1)S(1)}, u32[]{:S(2)}, u32[]{:S(2)}) collective-permute-start(bf16[64,3584]{1,0:T(8,128)(2,1)} %param.6), channel_id=1, source_target_pairs={{0,2},{2,0},{4,6},{6,4},{8,10},{10,8},{12,14},{14,12},{16,18},{18,... | collective-permute-start | bytes 1376264 | tf_op jit(solution)/shard_map/ppermute | solution.py:11
  20.3 21.4 %collective-permute-start.1 = (bf16[128,3584]{1,0:T(8,128)(2,1)S(1)}, bf16[128,3584]{1,0:T(8,128)(2,1)}, u32[]{:S(2)}, u32[]{:S(2)}) collective-permute-start(bf16[128,3584]{1,0:T(8,128)(2,1)S(1)} %maximum_select_fusion.3), channel_id=1, source_target_pairs={{0,4},{2,6},{4,0},{6,2},{8,12},{10,14},{12,8},{14,10},{16,20},{18,... | collective-permute-start | bytes 2752520 | tf_op jit(solution)/shard_map/ppermute | solution.py:11
  43.7 40.2 %collective-permute-start.2 = (bf16[256,3584]{1,0:T(8,128)(2,1)S(1)}, bf16[256,3584]{1,0:T(8,128)(2,1)}, u32[]{:S(2)}, u32[]{:S(2)}) collective-permute-start(bf16[256,3584]{1,0:T(8,128)(2,1)S(1)} %maximum_select_fusion.2), channel_id=1, source_target_pairs={{0,8},{2,10},{4,12},{6,14},{8,0},{10,2},{12,4},{14,6},{16,24},{18,... | collective-permute-start | bytes 5505032 | tf_op jit(solution)/shard_map/ppermute | solution.py:11
  87.7 157.5 %collective-permute-start.3 = (bf16[512,3584]{1,0:T(8,128)(2,1)}, bf16[512,3584]{1,0:T(8,128)(2,1)}, u32[]{:S(2)}, u32[]{:S(2)}) collective-permute-start(bf16[512,3584]{1,0:T(8,128)(2,1)} %maximum_select_fusion.1), channel_id=1, source_target_pairs={{0,16},{2,18},{4,20},{6,22},{8,24},{10,26},{12,28},{14,30},{16,0},... | collective-permute-start | bytes 11010056 | tf_op jit(solution)/shard_map/ppermute | solution.py:11
  270.0 22.6 %copy-start = (f32[64,8]{0,1:T(8,128)S(1)}, f32[64,8]{0,1:T(8,128)}, u32[]{:S(2)}) copy-start(f32[64,8]{0,1:T(8,128)} %param.8) | copy-start | bytes 6148
  270.0 22.6 %copy-start.1 = (s32[64,8]{0,1:T(8,128)S(1)}, s32[64,8]{0,1:T(8,128)}, u32[]{:S(2)}) copy-start(s32[64,8]{0,1:T(8,128)} %param.7) | copy-start | bytes 6148
  270.0 22.6 %copy-start.2 = (s32[16]{0:T(128)S(1)}, s32[16]{0:T(128)}, u32[]{:S(2)}) copy-start(s32[16]{0:T(128)} %param.9) | copy-start | bytes 196
  270.0 34.7 %all-gather.2.cloned.1.call-start = ((), (), s32[]{:S(2)}) async-start(), calls=%async_computation.4 | async-start | bytes 3145728 | tf_op jit(solution)/shard_map/all_gather | solution.py:81
  292.6 184.7 %reduce-scatter.5.cloned.1.call-start = ((), (), s32[]{:S(2)}) async-start(), calls=%async_computation.5 | async-start | bytes 7798784 | tf_op jit(solution)/shard_map/reduce_scatter | solution.py:86
Sparse Core Ops, SparseCore 0:
  270.1 18.5 reduce-scatter.2
  292.7 11.7 all-gather.1
  317.4 159.8 reduce-scatter.4
